TPU v7x, 1024 devices: a whole 8x8x8 slice. The times are simulated.
1024 devices in a mesh: tm: 16 (over x, core), seq: 8 (over y), mp: 8 (over z).
Axes of the slice: x: 8, y: 8, z: 8, core: 2. Of those that a mesh axis runs over, the one named last changes fastest.
Arguments:
- student_q: bfloat16 [8, 2048, 5120], P('seq', 'tm', 'mp'), may hold values from -110 to 110
- student_k: bfloat16 [8, 2048, 5120], P('seq', 'tm', 'mp'), may hold values from -6 to 6
- student_v: bfloat16 [8, 2048, 5120], P('seq', 'tm', 'mp'), may hold values from -6 to 6
- teacher_q: bfloat16 [8, 2048, 5120], P('seq', 'tm', 'mp'), may hold values from -110 to 110
- teacher_k: bfloat16 [8, 2048, 5120], P('seq', 'tm', 'mp'), may hold values from -6 to 6
- stagger: int32 [8], P('seq'), may hold values from 0 to 8, as said below
- clip_lengths: int32 [8, 3], P('seq'), may hold values from 1 to 9, 16 in all within a row
Outputs:
- generated: bfloat16 [8, 2048, 5120], P('seq', 'tm', 'mp')
- score_rows: bfloat16 [8, 2048, 5120], P('seq', 'tm', 'mp')
Inputs may be any that keep to these rules, and one draw needn't show every extreme that they name: `clip_lengths`: the lengths of each video sum to 16, and some clip has 9 blocks. `stagger`: some video has the value 16 // 2.
All inputs are finite; a program needn't handle non-finite values.
Results may differ from a plain program's by a relative error of at most 0.007.
Values may be sent and summed in bfloat16 or wider, within the bound.
A program may use at most 32 MiB of HBM per device.

v0:
```python
import math

import jax
import jax.numpy as jnp
from jax import lax
from jax.sharding import PartitionSpec as P

HD = 128
TOK = 128


negative = -1e30


def shifted(value, axis, by):
    peers = lax.axis_size(axis)
    pairs = [(i, i + by) for i in range(peers) if 0 <= i + by < peers]
    return lax.ppermute(value, axis, pairs)


def fold_piece(carry, queries, keys, values, allowed):
    top, total, acc = carry
    count = keys.shape[0]
    heads = queries.shape[1]
    kh = keys.reshape(count, heads, HD)
    vh = values.reshape(count, heads, HD)
    scores = jnp.einsum(
        "qhd,khd->hqk", queries, kh, preferred_element_type=jnp.float32
    ) / math.sqrt(HD)
    scores = jnp.where(allowed[None, None, :], scores, negative)
    new_top = jnp.maximum(top, jnp.max(scores, axis=-1))
    weights = jnp.where(allowed[None, None, :], jnp.exp(scores - new_top[..., None]), 0.0)
    factor = jnp.exp(top - new_top)
    total = total * factor + jnp.sum(weights, axis=-1)
    acc = acc * factor[..., None] + jnp.einsum(
        "hqk,khd->hqd", weights.astype(jnp.bfloat16), vh, preferred_element_type=jnp.float32
    )
    return (new_top, total, acc)


def masked_fold(carry, queries, keys, values, allowed):
    return fold_piece(carry, queries, keys, values, allowed)


def start_carry(heads):
    return (
        jnp.full((heads, TOK), negative, jnp.float32),
        jnp.zeros((heads, TOK), jnp.float32),
        jnp.zeros((heads, TOK, HD), jnp.float32),
    )


def finish(carry):
    top, total, acc = carry
    mixed = acc / total[..., None]
    return jnp.transpose(mixed, (1, 0, 2)).reshape(TOK, -1)


def per_device(student_q, student_k, student_v, teacher_q, teacher_k, stagger, clip_lengths):
    width = student_q.shape[2]
    heads = width // HD
    here = lax.axis_index("tm")
    first_block = stagger[0]
    block_count = lax.axis_size("tm")
    student_query_rows = student_q[0].reshape(TOK, heads, HD)

    def student_allowed(start, count):
        block = (start + jnp.arange(count, dtype=jnp.int32)) // TOK
        return (block == here) | (block >= first_block) & (block < here)

    def student_step(carry, keys, values, start):
        allowed = student_allowed(start, keys.shape[0])
        return masked_fold(carry, student_query_rows, keys, values, allowed)

    carry = student_step(start_carry(heads), student_k[0], student_v[0], here * TOK)

    def relay_turn(turn, state):
        inner, moving = state
        moving = shifted(moving, "tm", 1)
        inner = student_step(inner, moving[0], moving[1], (here - turn) * TOK)
        return (inner, moving)

    carry, unused = lax.fori_loop(
        1, block_count, relay_turn, (carry, jnp.stack([student_k[0], student_v[0]]))
    )
    generated = finish(carry).astype(jnp.bfloat16)[None]
    running = jnp.cumsum(clip_lengths[0])
    own_clip = jnp.sum((running <= here).astype(jnp.int32))
    teacher_query_rows = teacher_q[0].reshape(TOK, heads, HD)
    pieces = (
        lax.all_gather(teacher_k, "tm", axis=1, tiled=True),
        lax.all_gather(generated, "tm", axis=1, tiled=True),
    )
    count = pieces[0].shape[1]
    block = jnp.arange(count, dtype=jnp.int32) // TOK
    clip = jnp.sum((running[None, :] <= block[:, None]).astype(jnp.int32), axis=1)
    teacher_carry = masked_fold(
        start_carry(heads), teacher_query_rows, pieces[0][0], pieces[1][0], clip == own_clip
    )
    teacher_out = finish(teacher_carry)
    score_rows = (teacher_out - generated[0].astype(jnp.float32)).astype(jnp.bfloat16)[None]
    return (generated, score_rows)


def solution(mesh):
    in_specs = (
        P("seq", "tm", "mp"),
        P("seq", "tm", "mp"),
        P("seq", "tm", "mp"),
        P("seq", "tm", "mp"),
        P("seq", "tm", "mp"),
        P("seq"),
        P("seq", None),
    )
    out_specs = (P("seq", "tm", "mp"), P("seq", "tm", "mp"))
    return jax.shard_map(
        per_device, mesh=mesh, in_specs=in_specs, out_specs=out_specs, check_vma=False
    )
```

profile of v0, /device:TPU:1, one launch (start us, length us, event | category | flops | bytes accessed | tf_op | source)
XLA Modules:
  0.0 249.8 jit_solution(5891325467326852190)
XLA Ops:
  7.2 1.7 copy.52
  9.6 1.1 copy.40
  10.7 1.1 copy.41
  12.4 1.1 copy.44
  13.9 148.7 %while.21 = (s32[]{:T(128)}, f32[5,128]{1,0:T(8,128)S(1)}, f32[5,128]{1,0:T(8,128)S(1)}, f32[5,128,128]{2,1,0:T(8,128)S(1)}, bf16[2,128,640]{1,2,0:T(8,128)(2,1)...) while((s32[]{:T(128)}, f32[5,128]{1,0:T(8,128)S(1)}, ...), condition=%wide.region_5.6_spmd, body=%wide.region_2.5_spmd.sunk | while | flops 42848132 | bytes 4793009 | solution.py:83
  13.9 4.6 %collective-permute-start = (bf16[2,128,640]{1,2,0:T(8,128)(2,1)S(1)}, bf16[2,128,640]{1,2,0:T(8,128)(2,1)S(1)}, u32[]{:S(2)}, u32[]{:S(2)}) collective-permute-start(bf16[2,128,640]{1,2,0:T(8,128)(2,1)S(1)} %get-tuple-element.329), channel_id=1, source_target_pairs={{0,64},{64,128},{128,192},{192,256},{256,320},{320,384},{384,448},... | collective-permute-start | bytes 983048 | tf_op jit(solution)/shard_map/while/body/eval_jaxpr/ppermute | solution.py:18
  18.5 0.7 and_or_fusion.3
  19.2 11.3 %collective-permute-done = bf16[2,128,640]{1,2,0:T(8,128)(2,1)S(1)} collective-permute-done((bf16[2,128,640]{1,2,0:T(8,128)(2,1)S(1)}, bf16[2,128,640]{1,2,0:T(8,128)(2,1)S(1)}, u32[]{:S(2)}, u32[]{:S(2)}) %collective-permute-start) | collective-permute-done | bytes 327712 | tf_op jit(solution)/shard_map/while/body/eval_jaxpr/ppermute | solution.py:18
  31.4 1.9 collective-permute-start
  33.4 0.7 and_or_fusion.3
  34.0 3.3 %collective-permute-done = bf16[2,128,640]{1,2,0:T(8,128)(2,1)S(1)} collective-permute-done((bf16[2,128,640]{1,2,0:T(8,128)(2,1)S(1)}, bf16[2,128,640]{1,2,0:T(8,128)(2,1)S(1)}, u32[]{:S(2)}, u32[]{:S(2)}) %collective-permute-start) | collective-permute-done | bytes 327712 | tf_op jit(solution)/shard_map/while/body/eval_jaxpr/ppermute | solution.py:18
  38.2 4.4 %collective-permute-start = (bf16[2,128,640]{1,2,0:T(8,128)(2,1)S(1)}, bf16[2,128,640]{1,2,0:T(8,128)(2,1)S(1)}, u32[]{:S(2)}, u32[]{:S(2)}) collective-permute-start(bf16[2,128,640]{1,2,0:T(8,128)(2,1)S(1)} %get-tuple-element.329), channel_id=1, source_target_pairs={{0,64},{64,128},{128,192},{192,256},{256,320},{320,384},{384,448},... | collective-permute-start | bytes 983048 | tf_op jit(solution)/shard_map/while/body/eval_jaxpr/ppermute | solution.py:18
  42.6 0.7 and_or_fusion.3
  43.3 5.2 %collective-permute-done = bf16[2,128,640]{1,2,0:T(8,128)(2,1)S(1)} collective-permute-done((bf16[2,128,640]{1,2,0:T(8,128)(2,1)S(1)}, bf16[2,128,640]{1,2,0:T(8,128)(2,1)S(1)}, u32[]{:S(2)}, u32[]{:S(2)}) %collective-permute-start) | collective-permute-done | bytes 327712 | tf_op jit(solution)/shard_map/while/body/eval_jaxpr/ppermute | solution.py:18
  49.4 4.4 %collective-permute-start = (bf16[2,128,640]{1,2,0:T(8,128)(2,1)S(1)}, bf16[2,128,640]{1,2,0:T(8,128)(2,1)S(1)}, u32[]{:S(2)}, u32[]{:S(2)}) collective-permute-start(bf16[2,128,640]{1,2,0:T(8,128)(2,1)S(1)} %get-tuple-element.329), channel_id=1, source_target_pairs={{0,64},{64,128},{128,192},{192,256},{256,320},{320,384},{384,448},... | collective-permute-start | bytes 983048 | tf_op jit(solution)/shard_map/while/body/eval_jaxpr/ppermute | solution.py:18
  53.8 0.7 and_or_fusion.3
  54.5 5.1 %collective-permute-done = bf16[2,128,640]{1,2,0:T(8,128)(2,1)S(1)} collective-permute-done((bf16[2,128,640]{1,2,0:T(8,128)(2,1)S(1)}, bf16[2,128,640]{1,2,0:T(8,128)(2,1)S(1)}, u32[]{:S(2)}, u32[]{:S(2)}) %collective-permute-start) | collective-permute-done | bytes 327712 | tf_op jit(solution)/shard_map/while/body/eval_jaxpr/ppermute | solution.py:18
  60.5 4.4 %collective-permute-start = (bf16[2,128,640]{1,2,0:T(8,128)(2,1)S(1)}, bf16[2,128,640]{1,2,0:T(8,128)(2,1)S(1)}, u32[]{:S(2)}, u32[]{:S(2)}) collective-permute-start(bf16[2,128,640]{1,2,0:T(8,128)(2,1)S(1)} %get-tuple-element.329), channel_id=1, source_target_pairs={{0,64},{64,128},{128,192},{192,256},{256,320},{320,384},{384,448},... | collective-permute-start | bytes 983048 | tf_op jit(solution)/shard_map/while/body/eval_jaxpr/ppermute | solution.py:18
  64.9 0.7 and_or_fusion.3
  65.5 3.3 %collective-permute-done = bf16[2,128,640]{1,2,0:T(8,128)(2,1)S(1)} collective-permute-done((bf16[2,128,640]{1,2,0:T(8,128)(2,1)S(1)}, bf16[2,128,640]{1,2,0:T(8,128)(2,1)S(1)}, u32[]{:S(2)}, u32[]{:S(2)}) %collective-permute-start) | collective-permute-done | bytes 327712 | tf_op jit(solution)/shard_map/while/body/eval_jaxpr/ppermute | solution.py:18
  69.8 4.4 %collective-permute-start = (bf16[2,128,640]{1,2,0:T(8,128)(2,1)S(1)}, bf16[2,128,640]{1,2,0:T(8,128)(2,1)S(1)}, u32[]{:S(2)}, u32[]{:S(2)}) collective-permute-start(bf16[2,128,640]{1,2,0:T(8,128)(2,1)S(1)} %get-tuple-element.329), channel_id=1, source_target_pairs={{0,64},{64,128},{128,192},{192,256},{256,320},{320,384},{384,448},... | collective-permute-start | bytes 983048 | tf_op jit(solution)/shard_map/while/body/eval_jaxpr/ppermute | solution.py:18
  74.2 0.7 and_or_fusion.3
  74.8 3.3 %collective-permute-done = bf16[2,128,640]{1,2,0:T(8,128)(2,1)S(1)} collective-permute-done((bf16[2,128,640]{1,2,0:T(8,128)(2,1)S(1)}, bf16[2,128,640]{1,2,0:T(8,128)(2,1)S(1)}, u32[]{:S(2)}, u32[]{:S(2)}) %collective-permute-start) | collective-permute-done | bytes 327712 | tf_op jit(solution)/shard_map/while/body/eval_jaxpr/ppermute | solution.py:18
  79.0 4.4 %collective-permute-start = (bf16[2,128,640]{1,2,0:T(8,128)(2,1)S(1)}, bf16[2,128,640]{1,2,0:T(8,128)(2,1)S(1)}, u32[]{:S(2)}, u32[]{:S(2)}) collective-permute-start(bf16[2,128,640]{1,2,0:T(8,128)(2,1)S(1)} %get-tuple-element.329), channel_id=1, source_target_pairs={{0,64},{64,128},{128,192},{192,256},{256,320},{320,384},{384,448},... | collective-permute-start | bytes 983048 | tf_op jit(solution)/shard_map/while/body/eval_jaxpr/ppermute | solution.py:18
  83.4 0.7 and_or_fusion.3
  84.1 3.3 %collective-permute-done = bf16[2,128,640]{1,2,0:T(8,128)(2,1)S(1)} collective-permute-done((bf16[2,128,640]{1,2,0:T(8,128)(2,1)S(1)}, bf16[2,128,640]{1,2,0:T(8,128)(2,1)S(1)}, u32[]{:S(2)}, u32[]{:S(2)}) %collective-permute-start) | collective-permute-done | bytes 327712 | tf_op jit(solution)/shard_map/while/body/eval_jaxpr/ppermute | solution.py:18
  87.9 0.4 convolution_add_fusion.3
  88.3 4.4 %collective-permute-start = (bf16[2,128,640]{1,2,0:T(8,128)(2,1)S(1)}, bf16[2,128,640]{1,2,0:T(8,128)(2,1)S(1)}, u32[]{:S(2)}, u32[]{:S(2)}) collective-permute-start(bf16[2,128,640]{1,2,0:T(8,128)(2,1)S(1)} %get-tuple-element.329), channel_id=1, source_target_pairs={{0,64},{64,128},{128,192},{192,256},{256,320},{320,384},{384,448},... | collective-permute-start | bytes 983048 | tf_op jit(solution)/shard_map/while/body/eval_jaxpr/ppermute | solution.py:18
  92.7 0.7 and_or_fusion.3
  93.4 3.3 %collective-permute-done = bf16[2,128,640]{1,2,0:T(8,128)(2,1)S(1)} collective-permute-done((bf16[2,128,640]{1,2,0:T(8,128)(2,1)S(1)}, bf16[2,128,640]{1,2,0:T(8,128)(2,1)S(1)}, u32[]{:S(2)}, u32[]{:S(2)}) %collective-permute-start) | collective-permute-done | bytes 327712 | tf_op jit(solution)/shard_map/while/body/eval_jaxpr/ppermute | solution.py:18
  97.2 0.4 convolution_add_fusion.3
  97.6 4.4 %collective-permute-start = (bf16[2,128,640]{1,2,0:T(8,128)(2,1)S(1)}, bf16[2,128,640]{1,2,0:T(8,128)(2,1)S(1)}, u32[]{:S(2)}, u32[]{:S(2)}) collective-permute-start(bf16[2,128,640]{1,2,0:T(8,128)(2,1)S(1)} %get-tuple-element.329), channel_id=1, source_target_pairs={{0,64},{64,128},{128,192},{192,256},{256,320},{320,384},{384,448},... | collective-permute-start | bytes 983048 | tf_op jit(solution)/shard_map/while/body/eval_jaxpr/ppermute | solution.py:18
  102.0 0.7 and_or_fusion.3
  102.7 3.3 %collective-permute-done = bf16[2,128,640]{1,2,0:T(8,128)(2,1)S(1)} collective-permute-done((bf16[2,128,640]{1,2,0:T(8,128)(2,1)S(1)}, bf16[2,128,640]{1,2,0:T(8,128)(2,1)S(1)}, u32[]{:S(2)}, u32[]{:S(2)}) %collective-permute-start) | collective-permute-done | bytes 327712 | tf_op jit(solution)/shard_map/while/body/eval_jaxpr/ppermute | solution.py:18
  106.5 0.4 convolution_add_fusion.3
  106.9 4.4 %collective-permute-start = (bf16[2,128,640]{1,2,0:T(8,128)(2,1)S(1)}, bf16[2,128,640]{1,2,0:T(8,128)(2,1)S(1)}, u32[]{:S(2)}, u32[]{:S(2)}) collective-permute-start(bf16[2,128,640]{1,2,0:T(8,128)(2,1)S(1)} %get-tuple-element.329), channel_id=1, source_target_pairs={{0,64},{64,128},{128,192},{192,256},{256,320},{320,384},{384,448},... | collective-permute-start | bytes 983048 | tf_op jit(solution)/shard_map/while/body/eval_jaxpr/ppermute | solution.py:18
  111.3 0.7 and_or_fusion.3
  112.0 3.3 %collective-permute-done = bf16[2,128,640]{1,2,0:T(8,128)(2,1)S(1)} collective-permute-done((bf16[2,128,640]{1,2,0:T(8,128)(2,1)S(1)}, bf16[2,128,640]{1,2,0:T(8,128)(2,1)S(1)}, u32[]{:S(2)}, u32[]{:S(2)}) %collective-permute-start) | collective-permute-done | bytes 327712 | tf_op jit(solution)/shard_map/while/body/eval_jaxpr/ppermute | solution.py:18
  115.7 0.4 convolution_add_fusion.3
  116.2 4.4 %collective-permute-start = (bf16[2,128,640]{1,2,0:T(8,128)(2,1)S(1)}, bf16[2,128,640]{1,2,0:T(8,128)(2,1)S(1)}, u32[]{:S(2)}, u32[]{:S(2)}) collective-permute-start(bf16[2,128,640]{1,2,0:T(8,128)(2,1)S(1)} %get-tuple-element.329), channel_id=1, source_target_pairs={{0,64},{64,128},{128,192},{192,256},{256,320},{320,384},{384,448},... | collective-permute-start | bytes 983048 | tf_op jit(solution)/shard_map/while/body/eval_jaxpr/ppermute | solution.py:18
  120.6 0.7 and_or_fusion.3
  121.2 3.3 %collective-permute-done = bf16[2,128,640]{1,2,0:T(8,128)(2,1)S(1)} collective-permute-done((bf16[2,128,640]{1,2,0:T(8,128)(2,1)S(1)}, bf16[2,128,640]{1,2,0:T(8,128)(2,1)S(1)}, u32[]{:S(2)}, u32[]{:S(2)}) %collective-permute-start) | collective-permute-done | bytes 327712 | tf_op jit(solution)/shard_map/while/body/eval_jaxpr/ppermute | solution.py:18
  125.4 4.4 %collective-permute-start = (bf16[2,128,640]{1,2,0:T(8,128)(2,1)S(1)}, bf16[2,128,640]{1,2,0:T(8,128)(2,1)S(1)}, u32[]{:S(2)}, u32[]{:S(2)}) collective-permute-start(bf16[2,128,640]{1,2,0:T(8,128)(2,1)S(1)} %get-tuple-element.329), channel_id=1, source_target_pairs={{0,64},{64,128},{128,192},{192,256},{256,320},{320,384},{384,448},... | collective-permute-start | bytes 983048 | tf_op jit(solution)/shard_map/while/body/eval_jaxpr/ppermute | solution.py:18
  129.8 0.7 and_or_fusion.3
  130.5 3.3 %collective-permute-done = bf16[2,128,640]{1,2,0:T(8,128)(2,1)S(1)} collective-permute-done((bf16[2,128,640]{1,2,0:T(8,128)(2,1)S(1)}, bf16[2,128,640]{1,2,0:T(8,128)(2,1)S(1)}, u32[]{:S(2)}, u32[]{:S(2)}) %collective-permute-start) | collective-permute-done | bytes 327712 | tf_op jit(solution)/shard_map/while/body/eval_jaxpr/ppermute | solution.py:18
  134.7 4.4 %collective-permute-start = (bf16[2,128,640]{1,2,0:T(8,128)(2,1)S(1)}, bf16[2,128,640]{1,2,0:T(8,128)(2,1)S(1)}, u32[]{:S(2)}, u32[]{:S(2)}) collective-permute-start(bf16[2,128,640]{1,2,0:T(8,128)(2,1)S(1)} %get-tuple-element.329), channel_id=1, source_target_pairs={{0,64},{64,128},{128,192},{192,256},{256,320},{320,384},{384,448},... | collective-permute-start | bytes 983048 | tf_op jit(solution)/shard_map/while/body/eval_jaxpr/ppermute | solution.py:18
  139.1 0.7 and_or_fusion.3
  139.8 3.3 %collective-permute-done = bf16[2,128,640]{1,2,0:T(8,128)(2,1)S(1)} collective-permute-done((bf16[2,128,640]{1,2,0:T(8,128)(2,1)S(1)}, bf16[2,128,640]{1,2,0:T(8,128)(2,1)S(1)}, u32[]{:S(2)}, u32[]{:S(2)}) %collective-permute-start) | collective-permute-done | bytes 327712 | tf_op jit(solution)/shard_map/while/body/eval_jaxpr/ppermute | solution.py:18
  144.0 4.4 %collective-permute-start = (bf16[2,128,640]{1,2,0:T(8,128)(2,1)S(1)}, bf16[2,128,640]{1,2,0:T(8,128)(2,1)S(1)}, u32[]{:S(2)}, u32[]{:S(2)}) collective-permute-start(bf16[2,128,640]{1,2,0:T(8,128)(2,1)S(1)} %get-tuple-element.329), channel_id=1, source_target_pairs={{0,64},{64,128},{128,192},{192,256},{256,320},{320,384},{384,448},... | collective-permute-start | bytes 983048 | tf_op jit(solution)/shard_map/while/body/eval_jaxpr/ppermute | solution.py:18
  148.4 0.7 and_or_fusion.3
  149.1 3.3 %collective-permute-done = bf16[2,128,640]{1,2,0:T(8,128)(2,1)S(1)} collective-permute-done((bf16[2,128,640]{1,2,0:T(8,128)(2,1)S(1)}, bf16[2,128,640]{1,2,0:T(8,128)(2,1)S(1)}, u32[]{:S(2)}, u32[]{:S(2)}) %collective-permute-start) | collective-permute-done | bytes 327712 | tf_op jit(solution)/shard_map/while/body/eval_jaxpr/ppermute | solution.py:18
  153.3 4.4 %collective-permute-start = (bf16[2,128,640]{1,2,0:T(8,128)(2,1)S(1)}, bf16[2,128,640]{1,2,0:T(8,128)(2,1)S(1)}, u32[]{:S(2)}, u32[]{:S(2)}) collective-permute-start(bf16[2,128,640]{1,2,0:T(8,128)(2,1)S(1)} %get-tuple-element.329), channel_id=1, source_target_pairs={{0,64},{64,128},{128,192},{192,256},{256,320},{320,384},{384,448},... | collective-permute-start | bytes 983048 | tf_op jit(solution)/shard_map/while/body/eval_jaxpr/ppermute | solution.py:18
  157.7 0.7 and_or_fusion.3
  158.4 3.3 %collective-permute-done = bf16[2,128,640]{1,2,0:T(8,128)(2,1)S(1)} collective-permute-done((bf16[2,128,640]{1,2,0:T(8,128)(2,1)S(1)}, bf16[2,128,640]{1,2,0:T(8,128)(2,1)S(1)}, u32[]{:S(2)}, u32[]{:S(2)}) %collective-permute-start) | collective-permute-done | bytes 327712 | tf_op jit(solution)/shard_map/while/body/eval_jaxpr/ppermute | solution.py:18
  162.7 0.7 divide_convert_fusion
  163.5 1.7 copy.55
  165.5 0.6 fusion.34
  166.3 0.6 broadcast_compare_fusion
  166.9 2.9 %fusion.8 = (f32[5,128]{1,0:T(8,128)S(1)}, f32[5,128,2048]{2,1,0:T(8,128)S(1)}) fusion(pred[2048]{0:T(1024)(128)(4,1)S(1)} %broadcast_compare_fusion, bf16[128,5,128]{0,2,1:T(8,128)(2,1)S(1)} %bitcast.63, bf16[2048,5,128]{0,2,1:T(8,128)(2,1)} %bitcast.55), kind=kOutput, calls=%fused_computation.19 | convolution fusion | flops 339475840 | bytes 8032768 | tf_op jit(solution)/shard_map/qhd,khd->hqk/dot_general | solution.py:27
  169.8 2.3 copy-done
  172.1 1.3 fusion.9
  173.4 63.7 %all-gather.5.cloned.1.call-done = bf16[1,2048,640]{1,2,0:T(8,128)(2,1)} async-done(((bf16[1,128,640]{1,2,0:T(8,128)(2,1)}), bf16[1,2048,640]{1,2,0:T(8,128)(2,1)}) %all-gather.5.cloned.1.call-update) | async-done | bytes 2621456 | tf_op jit(solution)/shard_map/all_gather | solution.py:92
  237.1 5.0 %fusion.21 = f32[128,5,128]{0,2,1:T(8,128)S(1)} fusion(bf16[2048,5,128]{0,2,1:T(8,128)(2,1)} %bitcast.65, f32[5,128,2048]{2,1,0:T(8,128)} %copy-done, f32[5,128]{1,0:T(8,128)S(1)} %get-tuple-element.247, pred[2048]{0:T(1024)(128)(4,1)S(1)} %broadcast_compare_fusion, f32[128,5]{0,1:T(8,128)S(1)} %bitcast_add_fusion, f32[128,5]{0,1:T(8,128)S(1)} %get-tuple-element.246), kind=kOutput, calls=%fused_computation.29 | convolution fusion | flops 342261760 | bytes 8201728 | tf_op jit(solution)/shard_map/hqk,khd->hqd/dot_general | solution.py:35
  242.2 0.8 copy.56
  (144 shorter events, 12.7 us)
Async XLA Ops:
  7.2 159.7 %all-gather.3.cloned.1.call-start = ((), (), s32[]{:S(2)}) async-start(), calls=%async_computation | async-start | bytes 2785280 | tf_op jit(solution)/shard_map/all_gather | solution.py:91
  8.9 228.2 %all-gather.5.cloned.1.call-start = ((), (), s32[]{:S(2)}) async-start(), calls=%async_computation.1 | async-start | bytes 2785280 | tf_op jit(solution)/shard_map/all_gather | solution.py:92
  13.9 151.3 %copy-start.3 = (s32[1,3]{1,0:T(1,128)S(1)}, s32[1,3]{1,0:T(1,128)}, u32[]{:S(2)}) copy-start(s32[1,3]{1,0:T(1,128)} %param.15) | copy-start | bytes 40
  13.9 151.5 %copy-start.2 = (bf16[1,128,640]{2,1,0:T(8,128)(2,1)S(1)}, bf16[1,128,640]{2,1,0:T(8,128)(2,1)}, u32[]{:S(2)}) copy-start(bf16[1,128,640]{2,1,0:T(8,128)(2,1)} %param.12) | copy-start | bytes 491524
  13.9 16.6 %collective-permute-start = (bf16[2,128,640]{1,2,0:T(8,128)(2,1)S(1)}, bf16[2,128,640]{1,2,0:T(8,128)(2,1)S(1)}, u32[]{:S(2)}, u32[]{:S(2)}) collective-permute-start(bf16[2,128,640]{1,2,0:T(8,128)(2,1)S(1)} %get-tuple-element.329), channel_id=1, source_target_pairs={{0,64},{64,128},{128,192},{192,256},{256,320},{320,384},{384,448},... | collective-permute-start | bytes 983048 | tf_op jit(solution)/shard_map/while/body/eval_jaxpr/ppermute | solution.py:18
  31.4 5.9 %collective-permute-start = (bf16[2,128,640]{1,2,0:T(8,128)(2,1)S(1)}, bf16[2,128,640]{1,2,0:T(8,128)(2,1)S(1)}, u32[]{:S(2)}, u32[]{:S(2)}) collective-permute-start(bf16[2,128,640]{1,2,0:T(8,128)(2,1)S(1)} %get-tuple-element.329), channel_id=1, source_target_pairs={{0,64},{64,128},{128,192},{192,256},{256,320},{320,384},{384,448},... | collective-permute-start | bytes 983048 | tf_op jit(solution)/shard_map/while/body/eval_jaxpr/ppermute | solution.py:18
  38.2 10.3 %collective-permute-start = (bf16[2,128,640]{1,2,0:T(8,128)(2,1)S(1)}, bf16[2,128,640]{1,2,0:T(8,128)(2,1)S(1)}, u32[]{:S(2)}, u32[]{:S(2)}) collective-permute-start(bf16[2,128,640]{1,2,0:T(8,128)(2,1)S(1)} %get-tuple-element.329), channel_id=1, source_target_pairs={{0,64},{64,128},{128,192},{192,256},{256,320},{320,384},{384,448},... | collective-permute-start | bytes 983048 | tf_op jit(solution)/shard_map/while/body/eval_jaxpr/ppermute | solution.py:18
  49.4 10.2 %collective-permute-start = (bf16[2,128,640]{1,2,0:T(8,128)(2,1)S(1)}, bf16[2,128,640]{1,2,0:T(8,128)(2,1)S(1)}, u32[]{:S(2)}, u32[]{:S(2)}) collective-permute-start(bf16[2,128,640]{1,2,0:T(8,128)(2,1)S(1)} %get-tuple-element.329), channel_id=1, source_target_pairs={{0,64},{64,128},{128,192},{192,256},{256,320},{320,384},{384,448},... | collective-permute-start | bytes 983048 | tf_op jit(solution)/shard_map/while/body/eval_jaxpr/ppermute | solution.py:18
  60.5 8.4 %collective-permute-start = (bf16[2,128,640]{1,2,0:T(8,128)(2,1)S(1)}, bf16[2,128,640]{1,2,0:T(8,128)(2,1)S(1)}, u32[]{:S(2)}, u32[]{:S(2)}) collective-permute-start(bf16[2,128,640]{1,2,0:T(8,128)(2,1)S(1)} %get-tuple-element.329), channel_id=1, source_target_pairs={{0,64},{64,128},{128,192},{192,256},{256,320},{320,384},{384,448},... | collective-permute-start | bytes 983048 | tf_op jit(solution)/shard_map/while/body/eval_jaxpr/ppermute | solution.py:18
  69.8 8.4 %collective-permute-start = (bf16[2,128,640]{1,2,0:T(8,128)(2,1)S(1)}, bf16[2,128,640]{1,2,0:T(8,128)(2,1)S(1)}, u32[]{:S(2)}, u32[]{:S(2)}) collective-permute-start(bf16[2,128,640]{1,2,0:T(8,128)(2,1)S(1)} %get-tuple-element.329), channel_id=1, source_target_pairs={{0,64},{64,128},{128,192},{192,256},{256,320},{320,384},{384,448},... | collective-permute-start | bytes 983048 | tf_op jit(solution)/shard_map/while/body/eval_jaxpr/ppermute | solution.py:18
  79.0 8.4 %collective-permute-start = (bf16[2,128,640]{1,2,0:T(8,128)(2,1)S(1)}, bf16[2,128,640]{1,2,0:T(8,128)(2,1)S(1)}, u32[]{:S(2)}, u32[]{:S(2)}) collective-permute-start(bf16[2,128,640]{1,2,0:T(8,128)(2,1)S(1)} %get-tuple-element.329), channel_id=1, source_target_pairs={{0,64},{64,128},{128,192},{192,256},{256,320},{320,384},{384,448},... | collective-permute-start | bytes 983048 | tf_op jit(solution)/shard_map/while/body/eval_jaxpr/ppermute | solution.py:18
  88.3 8.4 %collective-permute-start = (bf16[2,128,640]{1,2,0:T(8,128)(2,1)S(1)}, bf16[2,128,640]{1,2,0:T(8,128)(2,1)S(1)}, u32[]{:S(2)}, u32[]{:S(2)}) collective-permute-start(bf16[2,128,640]{1,2,0:T(8,128)(2,1)S(1)} %get-tuple-element.329), channel_id=1, source_target_pairs={{0,64},{64,128},{128,192},{192,256},{256,320},{320,384},{384,448},... | collective-permute-start | bytes 983048 | tf_op jit(solution)/shard_map/while/body/eval_jaxpr/ppermute | solution.py:18
  97.6 8.4 %collective-permute-start = (bf16[2,128,640]{1,2,0:T(8,128)(2,1)S(1)}, bf16[2,128,640]{1,2,0:T(8,128)(2,1)S(1)}, u32[]{:S(2)}, u32[]{:S(2)}) collective-permute-start(bf16[2,128,640]{1,2,0:T(8,128)(2,1)S(1)} %get-tuple-element.329), channel_id=1, source_target_pairs={{0,64},{64,128},{128,192},{192,256},{256,320},{320,384},{384,448},... | collective-permute-start | bytes 983048 | tf_op jit(solution)/shard_map/while/body/eval_jaxpr/ppermute | solution.py:18
  106.9 8.4 %collective-permute-start = (bf16[2,128,640]{1,2,0:T(8,128)(2,1)S(1)}, bf16[2,128,640]{1,2,0:T(8,128)(2,1)S(1)}, u32[]{:S(2)}, u32[]{:S(2)}) collective-permute-start(bf16[2,128,640]{1,2,0:T(8,128)(2,1)S(1)} %get-tuple-element.329), channel_id=1, source_target_pairs={{0,64},{64,128},{128,192},{192,256},{256,320},{320,384},{384,448},... | collective-permute-start | bytes 983048 | tf_op jit(solution)/shard_map/while/body/eval_jaxpr/ppermute | solution.py:18
  116.2 8.4 %collective-permute-start = (bf16[2,128,640]{1,2,0:T(8,128)(2,1)S(1)}, bf16[2,128,640]{1,2,0:T(8,128)(2,1)S(1)}, u32[]{:S(2)}, u32[]{:S(2)}) collective-permute-start(bf16[2,128,640]{1,2,0:T(8,128)(2,1)S(1)} %get-tuple-element.329), channel_id=1, source_target_pairs={{0,64},{64,128},{128,192},{192,256},{256,320},{320,384},{384,448},... | collective-permute-start | bytes 983048 | tf_op jit(solution)/shard_map/while/body/eval_jaxpr/ppermute | solution.py:18
  125.4 8.4 %collective-permute-start = (bf16[2,128,640]{1,2,0:T(8,128)(2,1)S(1)}, bf16[2,128,640]{1,2,0:T(8,128)(2,1)S(1)}, u32[]{:S(2)}, u32[]{:S(2)}) collective-permute-start(bf16[2,128,640]{1,2,0:T(8,128)(2,1)S(1)} %get-tuple-element.329), channel_id=1, source_target_pairs={{0,64},{64,128},{128,192},{192,256},{256,320},{320,384},{384,448},... | collective-permute-start | bytes 983048 | tf_op jit(solution)/shard_map/while/body/eval_jaxpr/ppermute | solution.py:18
  134.7 8.4 %collective-permute-start = (bf16[2,128,640]{1,2,0:T(8,128)(2,1)S(1)}, bf16[2,128,640]{1,2,0:T(8,128)(2,1)S(1)}, u32[]{:S(2)}, u32[]{:S(2)}) collective-permute-start(bf16[2,128,640]{1,2,0:T(8,128)(2,1)S(1)} %get-tuple-element.329), channel_id=1, source_target_pairs={{0,64},{64,128},{128,192},{192,256},{256,320},{320,384},{384,448},... | collective-permute-start | bytes 983048 | tf_op jit(solution)/shard_map/while/body/eval_jaxpr/ppermute | solution.py:18
  144.0 8.4 %collective-permute-start = (bf16[2,128,640]{1,2,0:T(8,128)(2,1)S(1)}, bf16[2,128,640]{1,2,0:T(8,128)(2,1)S(1)}, u32[]{:S(2)}, u32[]{:S(2)}) collective-permute-start(bf16[2,128,640]{1,2,0:T(8,128)(2,1)S(1)} %get-tuple-element.329), channel_id=1, source_target_pairs={{0,64},{64,128},{128,192},{192,256},{256,320},{320,384},{384,448},... | collective-permute-start | bytes 983048 | tf_op jit(solution)/shard_map/while/body/eval_jaxpr/ppermute | solution.py:18
  153.3 8.4 %collective-permute-start = (bf16[2,128,640]{1,2,0:T(8,128)(2,1)S(1)}, bf16[2,128,640]{1,2,0:T(8,128)(2,1)S(1)}, u32[]{:S(2)}, u32[]{:S(2)}) collective-permute-start(bf16[2,128,640]{1,2,0:T(8,128)(2,1)S(1)} %get-tuple-element.329), channel_id=1, source_target_pairs={{0,64},{64,128},{128,192},{192,256},{256,320},{320,384},{384,448},... | collective-permute-start | bytes 983048 | tf_op jit(solution)/shard_map/while/body/eval_jaxpr/ppermute | solution.py:18
  169.8 2.3 copy-start
  237.1 5.0 %copy-start.1 = (bf16[5,128,128]{1,2,0:T(8,128)(2,1)S(1)}, bf16[5,128,128]{1,2,0:T(8,128)(2,1)}, u32[]{:S(2)}) copy-start(bf16[5,128,128]{1,2,0:T(8,128)(2,1)} %divide_convert_fusion) | copy-start | bytes 491524
Sparse Core Ops, SparseCore 0:
  10.6 64.3 all-gather.2
  163.6 73.4 all-gather.4
where the time goes:
time: 251 us; the launch traced here: 250 us
  waiting for transfers between devices  125 us (50%)
  starting transfers between devices  63.7 us (25%)
  matrix products  18.5 us (7%)
  other arithmetic  15.5 us (6%)
  between operations  14.8 us (6%)
  local copies, waits for them, and re-layouts  11 us (4%)
    all_gather x1, waiting for transfers between devices, per_device(): lax.all_gather(generated, 'tm', axis=1, tiled=True)  63.7 us
    ppermute x15, starting transfers between devices, shifted(): return lax.ppermute(value, axis, pairs)  63.6 us
    ppermute x15, waiting for transfers between devices, shifted(): return lax.ppermute(value, axis, pairs)  61.6 us
    dot_general x17, matrix products, fold_piece(): jnp.einsum('hqk,khd->hqd', weights.astype(jnp.bfloat16), vh, preferred_el...  10.9 us
    unnamed x15, local copies, waits for them, and re-layouts  9.95 us
    or x16, other arithmetic, student_allowed(): return (block == here) | (block >= first_block) & (block < here)  9.93 us
    dot_general x17, matrix products, fold_piece(): jnp.einsum('qhd,khd->hqk', queries, kh, preferred_element_type=jnp.float32)  7.54 us
  transfers between devices with their start and end apart: 17, of which 16 were waited for; matrix products, arithmetic and copies ran while one was open for 14% of the time, Pallas kernels for 0%

commit v1 on v0

v1 whole, which is shorter than its diff:
```python
import math

import jax
import jax.numpy as jnp
from jax import lax
from jax.experimental import pallas as pl
from jax.experimental.pallas import tpu as pltpu
from jax.sharding import PartitionSpec as P

HD = 128
TOK = 128
CHIPS = 8
HEADS = 5
BLOCKS = 16
MESH = pl.DeviceIdType.MESH
NEG = -1e30
FACTOR = math.log2(math.e) / math.sqrt(HD)
HOME = tuple(CHIPS * h // HEADS for h in range(HEADS))
ORDER = (0, 1, 7, 2, 6, 3, 5, 4)

Q, K, V, TQ, TK = range(5)
RELAYED = (K, V, TK)


def kernel(
    sq, sk, sv, tq, tk, stagger, clips, gen, score,
    qb, kb, vb, tqb, tkb, gb, sb, scores,
    send, recv, rel_send, rel_recv, gx_send, gx_recv, go_send, go_recv, so_send, so_recv,
):
    me = lax.axis_index("tm")
    x = me // 2
    c = lax.rem(me, 2)
    mine = (5 * x + 4) // CHIPS
    active = x == HOME[0]
    for h in range(1, HEADS):
        active = active | (x == HOME[h])
    inputs = (sq, sk, sv, tq, tk)
    buffers = (qb, kb, vb, tqb, tkb)
    other = {"tm": 2 * x + 1 - c}

    def rows(block):
        return pl.ds(pl.multiple_of(block * TOK, TOK), TOK)

    def head(h):
        return pl.ds(pl.multiple_of(h * HD, HD), HD)

    def place(a, chip, core):
        return buffers[a].at[rows(chip) if a in (Q, TQ) else rows(2 * chip + core)]

    barrier = pltpu.get_barrier_semaphore()
    for h in range(HEADS):
        @pl.when(x != HOME[h])
        def _():
            pl.semaphore_signal(barrier, inc=1, device_id={"tm": 2 * HOME[h] + c}, device_id_type=MESH)

    @pl.when(active)
    def _():
        for idle in range(CHIPS):
            if idle not in HOME:
                pl.semaphore_signal(barrier, inc=1, device_id={"tm": 2 * idle + c}, device_id_type=MESH)
        pl.semaphore_signal(barrier, inc=1, device_id=other, device_id_type=MESH)
        pl.semaphore_wait(barrier, CHIPS)

    @pl.when(jnp.logical_not(active))
    def _():
        pl.semaphore_wait(barrier, HEADS)

    def outgoing(a, h):
        return pltpu.make_async_remote_copy(
            src_ref=inputs[a].at[0, :, pl.ds(h * HD, HD)],
            dst_ref=place(a, x, c),
            send_sem=send.at[a, h],
            recv_sem=recv.at[a, x],
            device_id={"tm": 2 * HOME[h] + c},
            device_id_type=MESH,
        )

    for a in (K, Q, V, TQ, TK):
        for h in range(HEADS):
            @pl.when(x != HOME[h])
            def _():
                outgoing(a, h).start()

            @pl.when(x == HOME[h])
            def _():
                pltpu.make_async_copy(
                    inputs[a].at[0, :, pl.ds(h * HD, HD)], place(a, x, c), recv.at[a, x]
                ).start()

    def arrived(a, chip):
        pltpu.make_async_copy(place(a, chip, c), place(a, chip, c), recv.at[a, chip]).wait()

    def relay(a, chip):
        r = RELAYED.index(a)
        return pltpu.make_async_remote_copy(
            src_ref=place(a, chip, c),
            dst_ref=place(a, chip, c),
            send_sem=rel_send.at[r, chip],
            recv_sem=rel_recv.at[r, chip],
            device_id=other,
            device_id_type=MESH,
        )

    def relayed(a, chip):
        r = RELAYED.index(a)
        pltpu.make_async_copy(place(a, chip, 1 - c), place(a, chip, 1 - c), rel_recv.at[r, chip]).wait()

    def to_other(i):
        return pltpu.make_async_remote_copy(
            src_ref=gb.at[rows(2 * i + c)],
            dst_ref=gb.at[rows(2 * i + c)],
            send_sem=gx_send.at[i],
            recv_sem=gx_recv.at[i],
            device_id=other,
            device_id_type=MESH,
        )

    def to_owner(i, source, target, sends, recvs):
        return pltpu.make_async_remote_copy(
            src_ref=source,
            dst_ref=target.at[0, :, head(mine)],
            send_sem=sends.at[i],
            recv_sem=recvs.at[mine],
            device_id={"tm": 2 * i + c},
            device_id_type=MESH,
        )

    def hand_over(i, source, target, sends, recvs):
        @pl.when(x != i)
        def _():
            to_owner(i, source, target, sends, recvs).start()

        @pl.when(x == i)
        def _():
            pltpu.make_async_copy(source, target.at[0, :, head(mine)], recvs.at[mine]).start()

    def generated(i):
        return gb.at[rows(2 * i + c)]

    def scored(i):
        return sb.at[pl.ds(i * TOK, TOK)]

    def attend(queries, keys, values, tiles, bias):
        top = [None, None]
        for t in tiles:
            s = lax.dot_general(
                queries, keys[t * 256 : t * 256 + 256, :], (((1,), (1,)), ((), ())),
                preferred_element_type=jnp.float32,
            )
            for r in range(2):
                for u in range(2):
                    piece = s[r * TOK : r * TOK + TOK, u * TOK : u * TOK + TOK] + bias(r, 2 * t + u)
                    scores[r * TOK : r * TOK + TOK, (2 * t + u) * TOK : (2 * t + u + 1) * TOK] = piece
                    top[r] = piece if top[r] is None else jnp.maximum(top[r], piece)
        peak = jnp.concatenate([jnp.max(top[r], axis=1, keepdims=True) for r in range(2)], axis=0)
        total = jnp.zeros((2 * TOK, TOK), jnp.float32)
        acc = jnp.zeros((2 * TOK, HD), jnp.float32)
        for t in tiles:
            p = jnp.exp2((scores[:, t * 256 : t * 256 + 256] - peak) * FACTOR)
            total = total + (p[:, :TOK] + p[:, TOK:])
            acc = acc + jnp.dot(
                p.astype(jnp.bfloat16), values[t * 256 : t * 256 + 256, :],
                preferred_element_type=jnp.float32,
            )
        return acc / jnp.sum(total, axis=1, keepdims=True)

    @pl.when(active)
    def _():
        for d in ORDER:
            chip = lax.rem(x + d, CHIPS)
            for a in (K, Q, V):
                arrived(a, chip)
                if a in RELAYED:
                    relay(a, chip).start()
        for chip in range(CHIPS):
            relayed(K, chip)
            relayed(V, chip)

        first = stagger[0]
        for p in range(4):
            def student_bias(r, j):
                own = 2 * (2 * p + r) + c
                allowed = (j == own) | ((j >= first) & (j < own))
                return jnp.where(allowed, 0.0, NEG).astype(jnp.float32)

            mixed = attend(qb[p * 256 : p * 256 + 256, :], kb, vb, range(2 * p + 2), student_bias)
            mixed = mixed.astype(jnp.bfloat16)
            for r in range(2):
                gb[rows(2 * (2 * p + r) + c), :] = mixed[r * TOK : r * TOK + TOK, :]
            if p > 0:
                for i in (2 * p - 2, 2 * p - 1):
                    to_other(i).start()
                    hand_over(i, generated(i), gen, go_send, go_recv)

        for d in ORDER:
            chip = lax.rem(x + d, CHIPS)
            arrived(TQ, chip)
            arrived(TK, chip)
            relay(TK, chip).start()
            if d == 0:
                for i in (6, 7):
                    to_other(i).start()
                    hand_over(i, generated(i), gen, go_send, go_recv)
        for chip in range(CHIPS):
            relayed(TK, chip)
        for i in range(CHIPS):
            pltpu.make_async_copy(gb.at[rows(2 * i + 1 - c)], gb.at[rows(2 * i + 1 - c)], gx_recv.at[i]).wait()

        ends = [clips[0, 0], clips[0, 0] + clips[0, 1]]

        def clip_of(block):
            return (ends[0] <= block).astype(jnp.int32) + (ends[1] <= block).astype(jnp.int32)

        for p in range(4):
            def teacher_bias(r, j):
                same = clip_of(2 * (2 * p + r) + c) == clip_of(jnp.int32(j))
                return jnp.where(same, 0.0, NEG).astype(jnp.float32)

            tiles = range(max(0, 2 * p - 4), min(8, 2 * p + 6))
            mixed = attend(tqb[p * 256 : p * 256 + 256, :], tkb, gb, tiles, teacher_bias)
            for r in range(2):
                i = 2 * p + r
                own = gb[rows(2 * i + c), :].astype(jnp.float32)
                sb[i * TOK : i * TOK + TOK, :] = (mixed[r * TOK : r * TOK + TOK, :] - own).astype(jnp.bfloat16)
            if p > 0:
                for i in (2 * p - 2, 2 * p - 1):
                    hand_over(i, scored(i), score, so_send, so_recv)
        for i in (6, 7):
            hand_over(i, scored(i), score, so_send, so_recv)

        for chip in range(CHIPS):
            for a in RELAYED:
                relay(a, chip).wait_send()
            to_other(chip).wait_send()

            @pl.when(x != chip)
            def _():
                to_owner(chip, generated(chip), gen, go_send, go_recv).wait_send()
                to_owner(chip, scored(chip), score, so_send, so_recv).wait_send()

    for a in range(5):
        for h in range(HEADS):
            @pl.when(x != HOME[h])
            def _():
                outgoing(a, h).wait_send()

    for target, recvs in ((gen, go_recv), (score, so_recv)):
        for h in range(HEADS):
            spot = target.at[0, :, pl.ds(h * HD, HD)]
            pltpu.make_async_copy(spot, spot, recvs.at[h]).wait()


def per_device(student_q, student_k, student_v, teacher_q, teacher_k, stagger, clip_lengths):
    whole = jax.ShapeDtypeStruct(student_q.shape, jnp.bfloat16)
    anywhere = pl.BlockSpec(memory_space=pl.ANY)
    scalars = pl.BlockSpec(memory_space=pltpu.SMEM)
    half, full = (BLOCKS // 2 * TOK, HD), (BLOCKS * TOK, HD)
    dma = pltpu.SemaphoreType.DMA
    return pl.pallas_call(
        kernel,
        out_shape=(whole, whole),
        in_specs=[anywhere] * 5 + [scalars] * 2,
        out_specs=(anywhere, anywhere),
        scratch_shapes=[
            pltpu.VMEM(half, jnp.bfloat16),
            pltpu.VMEM(full, jnp.bfloat16),
            pltpu.VMEM(full, jnp.bfloat16),
            pltpu.VMEM(half, jnp.bfloat16),
            pltpu.VMEM(full, jnp.bfloat16),
            pltpu.VMEM(full, jnp.bfloat16),
            pltpu.VMEM(half, jnp.bfloat16),
            pltpu.VMEM((2 * TOK, BLOCKS * TOK), jnp.float32),
            dma((5, HEADS)),
            dma((5, CHIPS)),
            dma((3, CHIPS)),
            dma((3, CHIPS)),
            dma((CHIPS,)),
            dma((CHIPS,)),
            dma((CHIPS,)),
            dma((HEADS,)),
            dma((CHIPS,)),
            dma((HEADS,)),
        ],
        compiler_params=pltpu.CompilerParams(collective_id=0, has_side_effects=True),
        name="rollout",
    )(student_q, student_k, student_v, teacher_q, teacher_k, stagger, clip_lengths)


def solution(mesh):
    rows = P("seq", "tm", "mp")
    return jax.shard_map(
        per_device,
        mesh=mesh,
        in_specs=(rows,) * 5 + (P("seq"), P("seq", None)),
        out_specs=(rows, rows),
        check_vma=False,
    )
```

time: 251 us -> 51 us (0.20)
  the two profiles are of different devices: /device:TPU:1 before, /device:TPU:4 now
where the time goes in v1:
time: 51 us; the launch traced here: 50.8 us
  Pallas kernels  47.2 us (93%)
  local copies, waits for them, and re-layouts  2.3 us (5%)
  between operations  1.29 us (3%)
    pallas_call x1, Pallas kernels, per_device(): pl.pallas_call(kernel, out_shape=(whole, whole), in_specs=[anywhere] * 5...  47.2 us
    unnamed x4, local copies, waits for them, and re-layouts  2.3 us

profile of v1, /device:TPU:4, one launch (start us, length us, event | category | flops | bytes accessed | tf_op | source)
XLA Modules:
  0.0 50.8 jit_solution(919497487967328125)
XLA Ops:
  1.3 47.2 %rollout.1 = (bf16[1,128,640]{2,1,0:T(8,128)(2,1)}, bf16[1,128,640]{2,1,0:T(8,128)(2,1)}) custom-call(bf16[1,128,640]{2,1,0:T(8,128)(2,1)} %sq.1, bf16[1,128,640]{2,1,0:T(8,128)(2,1)} %sk.1, bf16[1,128,640]{2,1,0:T(8,128)(2,1)} %sv.1, bf16[1,128,640]{2,1,0:T(8,128)(2,1)} %tq.1, bf16[1,128,640]{2,1,0:T(8,128)(2,1)} %tk.1, s32[1]{0:T(128)S(6)} %copy.11.stagger, ...), custom_call_target="tpu_custom_call" | custom-call | tf_op jit(solution)/shard_map/rollout/pallas_call | solution.py:259
  48.4 0.0 copy-start
  48.5 1.6 %copy.12 = bf16[1,128,640]{2,1,0:T(8,128)(2,1)} copy(bf16[1,128,640]{2,1,0:T(8,128)(2,1)} %get-tuple-element.4) | data formatting | bytes 327680
  50.1 0.0 copy-done
  50.1 0.7 %copy.13 = bf16[1,128,640]{2,1,0:T(8,128)(2,1)} copy(bf16[1,128,640]{2,1,0:T(8,128)(2,1)S(1)} %copy-done) | data formatting | bytes 327680
Async XLA Ops:
  48.4 1.6 %copy-start = (bf16[1,128,640]{2,1,0:T(8,128)(2,1)S(1)}, bf16[1,128,640]{2,1,0:T(8,128)(2,1)}, u32[]{:S(2)}) copy-start(bf16[1,128,640]{2,1,0:T(8,128)(2,1)} %get-tuple-element.5) | copy-start | bytes 491524

commit v2 on v1

--- a/solution.py
+++ b/solution.py
@@ -15,7 +15,9 @@
 MESH = pl.DeviceIdType.MESH
 NEG = -1e30
 FACTOR = math.log2(math.e) / math.sqrt(HD)
-HOME = tuple(CHIPS * h // HEADS for h in range(HEADS))
+HOME = (0, 2, 3, 5, 6)
+LATE = ((0,), (3, 5))
+IDLE = tuple(chip for chip in range(CHIPS) if chip not in HOME)
 ORDER = (0, 1, 7, 2, 6, 3, 5, 4)
 
 Q, K, V, TQ, TK = range(5)
@@ -25,15 +27,23 @@
 def kernel(
     sq, sk, sv, tq, tk, stagger, clips, gen, score,
     qb, kb, vb, tqb, tkb, gb, sb, scores,
-    send, recv, rel_send, rel_recv, gx_send, gx_recv, go_send, go_recv, so_send, so_recv,
+    send, recv, rel_send, rel_recv, gx_send, gx_recv, go_send, go_recv, so_send, so_recv, ready, settled,
 ):
     me = lax.axis_index("tm")
     x = me // 2
     c = lax.rem(me, 2)
-    mine = (5 * x + 4) // CHIPS
+    mine = sum(h * (x == HOME[h]).astype(jnp.int32) for h in range(HEADS))
+    corner = (lax.axis_index("seq") == 0) & (lax.axis_index("mp") == 0)
+
+    def late(h):
+        return (corner & (HOME[h] in LATE[0])) | (jnp.logical_not(corner) & (HOME[h] in LATE[1]))
+
+    lates = jnp.where(corner, len(LATE[0]), len(LATE[1]))
     active = x == HOME[0]
+    last = (x == HOME[0]) & late(0)
     for h in range(1, HEADS):
         active = active | (x == HOME[h])
+        last = last | ((x == HOME[h]) & late(h))
     inputs = (sq, sk, sv, tq, tk)
     buffers = (qb, kb, vb, tqb, tkb)
     other = {"tm": 2 * x + 1 - c}
@@ -48,22 +58,37 @@
         return buffers[a].at[rows(chip) if a in (Q, TQ) else rows(2 * chip + core)]
 
     barrier = pltpu.get_barrier_semaphore()
-    for h in range(HEADS):
-        @pl.when(x != HOME[h])
-        def _():
-            pl.semaphore_signal(barrier, inc=1, device_id={"tm": 2 * HOME[h] + c}, device_id_type=MESH)
+    early = active & jnp.logical_not(last)
+
+    def greet(chip):
+        pl.semaphore_signal(barrier, inc=1, device_id={"tm": 2 * chip + c}, device_id_type=MESH)
+
+    @pl.when(early)
+    def _():
+        for d in ORDER[1:]:
+            greet(lax.rem(x + d, CHIPS))
+
+    @pl.when(jnp.logical_not(early))
+    def _():
+        for h in range(HEADS):
+            @pl.when((x != HOME[h]) & late(h))
+            def _():
+                greet(HOME[h])
 
     @pl.when(active)
     def _():
-        for idle in range(CHIPS):
-            if idle not in HOME:
-                pl.semaphore_signal(barrier, inc=1, device_id={"tm": 2 * idle + c}, device_id_type=MESH)
         pl.semaphore_signal(barrier, inc=1, device_id=other, device_id_type=MESH)
-        pl.semaphore_wait(barrier, CHIPS)
-
-    @pl.when(jnp.logical_not(active))
-    def _():
-        pl.semaphore_wait(barrier, HEADS)
+
+    pl.semaphore_wait(barrier, jnp.where(last, CHIPS, HEADS - lates))
+
+    @pl.when(last)
+    def _():
+        for chip in IDLE:
+            pl.semaphore_signal(settled, inc=1, device_id={"tm": 2 * chip + c}, device_id_type=MESH)
+        for h in range(HEADS):
+            @pl.when(jnp.logical_not(late(h)))
+            def _():
+                pl.semaphore_signal(settled, inc=1, device_id={"tm": 2 * HOME[h] + c}, device_id_type=MESH)
 
     def outgoing(a, h):
         return pltpu.make_async_remote_copy(
@@ -75,17 +100,34 @@
             device_id_type=MESH,
         )
 
-    for a in (K, Q, V, TQ, TK):
-        for h in range(HEADS):
-            @pl.when(x != HOME[h])
-            def _():
-                outgoing(a, h).start()
-
-            @pl.when(x == HOME[h])
-            def _():
-                pltpu.make_async_copy(
-                    inputs[a].at[0, :, pl.ds(h * HD, HD)], place(a, x, c), recv.at[a, x]
-                ).start()
+    def submit(arrays, chosen):
+        for a in arrays:
+            for h in range(HEADS):
+                @pl.when((x != HOME[h]) & chosen(h))
+                def _():
+                    outgoing(a, h).start()
+
+                @pl.when((x == HOME[h]) & chosen(h))
+                def _():
+                    pltpu.make_async_copy(
+                        inputs[a].at[0, :, pl.ds(h * HD, HD)], place(a, x, c), recv.at[a, x]
+                    ).start()
+
+    submit((K, Q, V), lambda h: jnp.logical_not(late(h)))
+
+    @pl.when(jnp.logical_not(active))
+    def _():
+        for h in range(HEADS):
+            @pl.when(jnp.logical_not(late(h)))
+            def _():
+                pl.semaphore_signal(ready, inc=1, device_id={"tm": 2 * HOME[h] + c}, device_id_type=MESH)
+
+    @pl.when(jnp.logical_not(last))
+    def _():
+        pl.semaphore_wait(settled, lates)
+
+    submit((K, Q, V), late)
+    submit((TQ, TK), lambda h: True)
 
     def arrived(a, chip):
         pltpu.make_async_copy(place(a, chip, c), place(a, chip, c), recv.at[a, chip]).wait()
@@ -176,6 +218,10 @@
             relayed(K, chip)
             relayed(V, chip)
 
+        @pl.when(early)
+        def _():
+            pl.semaphore_wait(ready, len(IDLE))
+
         first = stagger[0]
         for p in range(4):
             def student_bias(r, j):
@@ -211,7 +257,7 @@
         def clip_of(block):
             return (ends[0] <= block).astype(jnp.int32) + (ends[1] <= block).astype(jnp.int32)
 
-        for p in range(4):
+        for p in (0, 3, 1, 2):
             def teacher_bias(r, j):
                 same = clip_of(2 * (2 * p + r) + c) == clip_of(jnp.int32(j))
                 return jnp.where(same, 0.0, NEG).astype(jnp.float32)
@@ -222,11 +268,8 @@
                 i = 2 * p + r
                 own = gb[rows(2 * i + c), :].astype(jnp.float32)
                 sb[i * TOK : i * TOK + TOK, :] = (mixed[r * TOK : r * TOK + TOK, :] - own).astype(jnp.bfloat16)
-            if p > 0:
-                for i in (2 * p - 2, 2 * p - 1):
-                    hand_over(i, scored(i), score, so_send, so_recv)
-        for i in (6, 7):
-            hand_over(i, scored(i), score, so_send, so_recv)
+            for i in (2 * p, 2 * p + 1):
+                hand_over(i, scored(i), score, so_send, so_recv)
 
         for chip in range(CHIPS):
             for a in RELAYED:
@@ -248,6 +291,15 @@
         for h in range(HEADS):
             spot = target.at[0, :, pl.ds(h * HD, HD)]
             pltpu.make_async_copy(spot, spot, recvs.at[h]).wait()
+
+
+def settle(a, b, c, d, sems):
+    one = pltpu.make_async_copy(a, c, sems.at[0])
+    two = pltpu.make_async_copy(b, d, sems.at[1])
+    one.start()
+    two.start()
+    one.wait()
+    two.wait()
 
 
 def per_device(student_q, student_k, student_v, teacher_q, teacher_k, stagger, clip_lengths):
@@ -256,7 +308,7 @@
     scalars = pl.BlockSpec(memory_space=pltpu.SMEM)
     half, full = (BLOCKS // 2 * TOK, HD), (BLOCKS * TOK, HD)
     dma = pltpu.SemaphoreType.DMA
-    return pl.pallas_call(
+    outs = pl.pallas_call(
         kernel,
         out_shape=(whole, whole),
         in_specs=[anywhere] * 5 + [scalars] * 2,
@@ -280,10 +332,20 @@
             dma((HEADS,)),
             dma((CHIPS,)),
             dma((HEADS,)),
+            pltpu.SemaphoreType.REGULAR,
+            pltpu.SemaphoreType.REGULAR,
         ],
         compiler_params=pltpu.CompilerParams(collective_id=0, has_side_effects=True),
         name="rollout",
     )(student_q, student_k, student_v, teacher_q, teacher_k, stagger, clip_lengths)
+    return pl.pallas_call(
+        settle,
+        out_shape=(whole, whole),
+        in_specs=[pl.BlockSpec(memory_space=pltpu.VMEM)] * 2,
+        out_specs=(anywhere, anywhere),
+        scratch_shapes=[dma((2,))],
+        name="settle",
+    )(*outs)
 
 
 def solution(mesh):

time: 51 us -> 54.5 us (1.069)
  the two profiles are of different devices: /device:TPU:4 before, /device:TPU:8 now
where the time goes in v2:
time: 54.5 us; the launch traced here: 54.3 us
  Pallas kernels  53 us (97%)
  between operations  1.29 us (2%)
    pallas_call x1, Pallas kernels, per_device(): pl.pallas_call(kernel, out_shape=(whole, whole), in_specs=[anywhere] * 5...  51.2 us
    pallas_call x1, Pallas kernels, per_device(): pl.pallas_call(settle, out_shape=(whole, whole), in_specs=[pl.BlockSpec(m...  1.73 us

profile of v2, /device:TPU:8, one launch (start us, length us, event | category | flops | bytes accessed | tf_op | source)
XLA Modules:
  0.0 54.3 jit_solution(4721243365925733640)
XLA Ops:
  1.3 51.2 %rollout.1 = (bf16[1,128,640]{2,1,0:T(8,128)(2,1)}, bf16[1,128,640]{2,1,0:T(8,128)(2,1)}) custom-call(bf16[1,128,640]{2,1,0:T(8,128)(2,1)} %sq.1, bf16[1,128,640]{2,1,0:T(8,128)(2,1)} %sk.1, bf16[1,128,640]{2,1,0:T(8,128)(2,1)} %sv.1, bf16[1,128,640]{2,1,0:T(8,128)(2,1)} %tq.1, bf16[1,128,640]{2,1,0:T(8,128)(2,1)} %tk.1, s32[1]{0:T(128)S(6)} %copy.9.stagger, ...), custom_call_target="tpu_custom_call" | custom-call | tf_op jit(solution)/shard_map/rollout/pallas_call | solution.py:311
  52.5 1.7 %settle.1 = (bf16[1,128,640]{2,1,0:T(8,128)(2,1)}, bf16[1,128,640]{2,1,0:T(8,128)(2,1)}) custom-call(bf16[1,128,640]{2,1,0:T(8,128)(2,1)} %get-tuple-element.4.a, bf16[1,128,640]{2,1,0:T(8,128)(2,1)} %get-tuple-element.5.b), custom_call_target="tpu_custom_call" | custom-call | tf_op jit(solution)/shard_map/settle/pallas_call | solution.py:341

commit v3 on v2

--- a/solution.py
+++ b/solution.py
@@ -27,7 +27,7 @@
 def kernel(
     sq, sk, sv, tq, tk, stagger, clips, gen, score,
     qb, kb, vb, tqb, tkb, gb, sb, scores,
-    send, recv, rel_send, rel_recv, gx_send, gx_recv, go_send, go_recv, so_send, so_recv, ready, settled,
+    send, recv, rel_send, rel_recv, gx_send, gx_recv, go_send, go_recv, so_send, so_recv, ready, settled, paired,
 ):
     me = lax.axis_index("tm")
     x = me // 2
@@ -75,11 +75,16 @@
             def _():
                 greet(HOME[h])
 
-    @pl.when(active)
+    @pl.when(active & (c == 1))
     def _():
         pl.semaphore_signal(barrier, inc=1, device_id=other, device_id_type=MESH)
 
-    pl.semaphore_wait(barrier, jnp.where(last, CHIPS, HEADS - lates))
+    pairing = (active & (c == 0)).astype(jnp.int32)
+    pl.semaphore_wait(barrier, jnp.where(last, CHIPS - 1, HEADS - lates - early.astype(jnp.int32)) + pairing)
+
+    @pl.when(active & (c == 0))
+    def _():
+        pl.semaphore_signal(paired, inc=1, device_id=other, device_id_type=MESH)
 
     @pl.when(last)
     def _():
@@ -208,6 +213,10 @@
 
     @pl.when(active)
     def _():
+        @pl.when(c == 1)
+        def _():
+            pl.semaphore_wait(paired, 1)
+
         for d in ORDER:
             chip = lax.rem(x + d, CHIPS)
             for a in (K, Q, V):
@@ -334,6 +343,7 @@
             dma((HEADS,)),
             pltpu.SemaphoreType.REGULAR,
             pltpu.SemaphoreType.REGULAR,
+            pltpu.SemaphoreType.REGULAR,
         ],
         compiler_params=pltpu.CompilerParams(collective_id=0, has_side_effects=True),
         name="rollout",

time: 54.5 us -> 47.9 us (0.88)
  the two profiles are of different devices: /device:TPU:8 before, /device:TPU:4 now
where the time goes in v3:
time: 47.9 us; the launch traced here: 47.7 us
  Pallas kernels  46.4 us (97%)
  between operations  1.29 us (3%)
    pallas_call x1, Pallas kernels, per_device(): pl.pallas_call(kernel, out_shape=(whole, whole), in_specs=[anywhere] * 5...  44.6 us
    pallas_call x1, Pallas kernels, per_device(): pl.pallas_call(settle, out_shape=(whole, whole), in_specs=[pl.BlockSpec(m...  1.73 us

profile of v3, /device:TPU:4, one launch (start us, length us, event | category | flops | bytes accessed | tf_op | source)
XLA Modules:
  0.0 47.7 jit_solution(17616662147034547823)
XLA Ops:
  1.3 44.6 %rollout.1 = (bf16[1,128,640]{2,1,0:T(8,128)(2,1)}, bf16[1,128,640]{2,1,0:T(8,128)(2,1)}) custom-call(bf16[1,128,640]{2,1,0:T(8,128)(2,1)} %sq.1, bf16[1,128,640]{2,1,0:T(8,128)(2,1)} %sk.1, bf16[1,128,640]{2,1,0:T(8,128)(2,1)} %sv.1, bf16[1,128,640]{2,1,0:T(8,128)(2,1)} %tq.1, bf16[1,128,640]{2,1,0:T(8,128)(2,1)} %tk.1, s32[1]{0:T(128)S(6)} %copy.9.stagger, ...), custom_call_target="tpu_custom_call" | custom-call | tf_op jit(solution)/shard_map/rollout/pallas_call | solution.py:320
  45.9 1.7 %settle.1 = (bf16[1,128,640]{2,1,0:T(8,128)(2,1)}, bf16[1,128,640]{2,1,0:T(8,128)(2,1)}) custom-call(bf16[1,128,640]{2,1,0:T(8,128)(2,1)} %get-tuple-element.4.a, bf16[1,128,640]{2,1,0:T(8,128)(2,1)} %get-tuple-element.5.b), custom_call_target="tpu_custom_call" | custom-call | tf_op jit(solution)/shard_map/settle/pallas_call | solution.py:351

commit v4 on v3

--- a/solution.py
+++ b/solution.py
@@ -317,11 +317,12 @@
     scalars = pl.BlockSpec(memory_space=pltpu.SMEM)
     half, full = (BLOCKS // 2 * TOK, HD), (BLOCKS * TOK, HD)
     dma = pltpu.SemaphoreType.DMA
+    landing = pltpu.VMEM(student_q.shape, jnp.bfloat16)
     outs = pl.pallas_call(
         kernel,
-        out_shape=(whole, whole),
+        out_shape=(landing, landing),
         in_specs=[anywhere] * 5 + [scalars] * 2,
-        out_specs=(anywhere, anywhere),
+        out_specs=(pl.BlockSpec(memory_space=pltpu.VMEM),) * 2,
         scratch_shapes=[
             pltpu.VMEM(half, jnp.bfloat16),
             pltpu.VMEM(full, jnp.bfloat16),
@@ -355,7 +356,7 @@
         out_specs=(anywhere, anywhere),
         scratch_shapes=[dma((2,))],
         name="settle",
-    )(*outs)
+    )(*[pltpu.with_memory_space_constraint(rows, pltpu.VMEM) for rows in outs])
 
 
 def solution(mesh):

time: 47.9 us -> 46.8 us (0.977)
  Pallas kernels: 46.4 us -> 45.3 us
    pallas_call x1, Pallas kernels: 1.73 us -> 0.74 us  [per_device(): pl.pallas_call(settle, out_shape=(whole, whole), in_specs=[pl.BlockSpec(m...]
where the time goes in v4:
time: 46.8 us; the launch traced here: 46.6 us
  Pallas kernels  45.3 us (97%)
  between operations  1.29 us (3%)
    pallas_call x1, Pallas kernels, per_device(): pl.pallas_call(kernel, out_shape=(landing, landing), in_specs=[anywhere]...  44.5 us

profile of v4, /device:TPU:4, one launch (start us, length us, event | category | flops | bytes accessed | tf_op | source)
XLA Modules:
  0.0 46.6 jit_solution(14330239835178111682)
XLA Ops:
  1.3 44.5 %rollout.1 = (bf16[1,128,640]{2,1,0:T(8,128)(2,1)S(1)}, bf16[1,128,640]{2,1,0:T(8,128)(2,1)S(1)}) custom-call(bf16[1,128,640]{2,1,0:T(8,128)(2,1)} %sq.1, bf16[1,128,640]{2,1,0:T(8,128)(2,1)} %sk.1, bf16[1,128,640]{2,1,0:T(8,128)(2,1)} %sv.1, bf16[1,128,640]{2,1,0:T(8,128)(2,1)} %tq.1, bf16[1,128,640]{2,1,0:T(8,128)(2,1)} %tk.1, s32[1]{0:T(128)S(6)} %copy.9.stagger, ...), custom_call_target="tpu_custom_call" | custom-call | tf_op jit(solution)/shard_map/rollout/pallas_call | solution.py:321
  45.8 0.7 %settle.1 = (bf16[1,128,640]{2,1,0:T(8,128)(2,1)}, bf16[1,128,640]{2,1,0:T(8,128)(2,1)}) custom-call(bf16[1,128,640]{2,1,0:T(8,128)(2,1)S(1)} %get-tuple-element.4.a, bf16[1,128,640]{2,1,0:T(8,128)(2,1)S(1)} %get-tuple-element.5.b), custom_call_target="tpu_custom_call" | custom-call | tf_op jit(solution)/shard_map/settle/pallas_call | solution.py:352

commit v5 on v4

--- a/solution.py
+++ b/solution.py
@@ -35,15 +35,20 @@
     mine = sum(h * (x == HOME[h]).astype(jnp.int32) for h in range(HEADS))
     corner = (lax.axis_index("seq") == 0) & (lax.axis_index("mp") == 0)
 
-    def late(h):
-        return (corner & (HOME[h] in LATE[0])) | (jnp.logical_not(corner) & (HOME[h] in LATE[1]))
+    def late(chip):
+        there, elsewhere = [chip == LATE[0][0], chip == LATE[1][0]]
+        for other_chip in LATE[0][1:]:
+            there = there | (chip == other_chip)
+        for other_chip in LATE[1][1:]:
+            elsewhere = elsewhere | (chip == other_chip)
+        return (corner & there) | (jnp.logical_not(corner) & elsewhere)
 
     lates = jnp.where(corner, len(LATE[0]), len(LATE[1]))
     active = x == HOME[0]
-    last = (x == HOME[0]) & late(0)
+    last = (x == HOME[0]) & late(HOME[0])
     for h in range(1, HEADS):
         active = active | (x == HOME[h])
-        last = last | ((x == HOME[h]) & late(h))
+        last = last | ((x == HOME[h]) & late(HOME[h]))
     inputs = (sq, sk, sv, tq, tk)
     buffers = (qb, kb, vb, tqb, tkb)
     other = {"tm": 2 * x + 1 - c}
@@ -71,7 +76,7 @@
     @pl.when(jnp.logical_not(early))
     def _():
         for h in range(HEADS):
-            @pl.when((x != HOME[h]) & late(h))
+            @pl.when((x != HOME[h]) & late(HOME[h]))
             def _():
                 greet(HOME[h])
 
@@ -91,39 +96,44 @@
         for chip in IDLE:
             pl.semaphore_signal(settled, inc=1, device_id={"tm": 2 * chip + c}, device_id_type=MESH)
         for h in range(HEADS):
-            @pl.when(jnp.logical_not(late(h)))
+            @pl.when(jnp.logical_not(late(HOME[h])))
             def _():
                 pl.semaphore_signal(settled, inc=1, device_id={"tm": 2 * HOME[h] + c}, device_id_type=MESH)
 
-    def outgoing(a, h):
+    def outgoing(a, h, home):
         return pltpu.make_async_remote_copy(
-            src_ref=inputs[a].at[0, :, pl.ds(h * HD, HD)],
+            src_ref=inputs[a].at[0, :, head(h)],
             dst_ref=place(a, x, c),
             send_sem=send.at[a, h],
             recv_sem=recv.at[a, x],
-            device_id={"tm": 2 * HOME[h] + c},
+            device_id={"tm": 2 * home + c},
             device_id_type=MESH,
         )
 
+    far = (5 * lax.rem(x + 4, CHIPS) + 5) // CHIPS
+
     def submit(arrays, chosen):
         for a in arrays:
-            for h in range(HEADS):
-                @pl.when((x != HOME[h]) & chosen(h))
+            for step in (0, 4, 1, 3, 2):
+                h = lax.rem(far + step, HEADS)
+                home = (CHIPS * h + 2) // HEADS
+
+                @pl.when((x != home) & chosen(home))
                 def _():
-                    outgoing(a, h).start()
-
-                @pl.when((x == HOME[h]) & chosen(h))
+                    outgoing(a, h, home).start()
+
+                @pl.when((x == home) & chosen(home))
                 def _():
                     pltpu.make_async_copy(
-                        inputs[a].at[0, :, pl.ds(h * HD, HD)], place(a, x, c), recv.at[a, x]
+                        inputs[a].at[0, :, head(h)], place(a, x, c), recv.at[a, x]
                     ).start()
 
-    submit((K, Q, V), lambda h: jnp.logical_not(late(h)))
+    submit((K, Q, V), lambda home: jnp.logical_not(late(home)))
 
     @pl.when(jnp.logical_not(active))
     def _():
         for h in range(HEADS):
-            @pl.when(jnp.logical_not(late(h)))
+            @pl.when(jnp.logical_not(late(HOME[h])))
             def _():
                 pl.semaphore_signal(ready, inc=1, device_id={"tm": 2 * HOME[h] + c}, device_id_type=MESH)
 
@@ -132,7 +142,7 @@
         pl.semaphore_wait(settled, lates)
 
     submit((K, Q, V), late)
-    submit((TQ, TK), lambda h: True)
+    submit((TQ, TK), lambda home: True)
 
     def arrived(a, chip):
         pltpu.make_async_copy(place(a, chip, c), place(a, chip, c), recv.at[a, chip]).wait()
@@ -294,7 +304,7 @@
         for h in range(HEADS):
             @pl.when(x != HOME[h])
             def _():
-                outgoing(a, h).wait_send()
+                outgoing(a, h, HOME[h]).wait_send()
 
     for target, recvs in ((gen, go_recv), (score, so_recv)):
         for h in range(HEADS):

time: 46.8 us -> 46.9 us (level)
  no operation moved by 1% of the time
where the time goes in v5:
time: 46.9 us; the launch traced here: 46.7 us
  Pallas kernels  45.4 us (97%)
  between operations  1.29 us (3%)
    pallas_call x1, Pallas kernels, per_device(): pl.pallas_call(kernel, out_shape=(landing, landing), in_specs=[anywhere]...  44.6 us

profile of v5, /device:TPU:4, one launch (start us, length us, event | category | flops | bytes accessed | tf_op | source)
XLA Modules:
  0.0 46.7 jit_solution(4274254846039841097)
XLA Ops:
  1.3 44.6 %rollout.1 = (bf16[1,128,640]{2,1,0:T(8,128)(2,1)S(1)}, bf16[1,128,640]{2,1,0:T(8,128)(2,1)S(1)}) custom-call(bf16[1,128,640]{2,1,0:T(8,128)(2,1)} %sq.1, bf16[1,128,640]{2,1,0:T(8,128)(2,1)} %sk.1, bf16[1,128,640]{2,1,0:T(8,128)(2,1)} %sv.1, bf16[1,128,640]{2,1,0:T(8,128)(2,1)} %tq.1, bf16[1,128,640]{2,1,0:T(8,128)(2,1)} %tk.1, s32[1]{0:T(128)S(6)} %copy.9.stagger, ...), custom_call_target="tpu_custom_call" | custom-call | tf_op jit(solution)/shard_map/rollout/pallas_call | solution.py:331
  45.9 0.7 %settle.1 = (bf16[1,128,640]{2,1,0:T(8,128)(2,1)}, bf16[1,128,640]{2,1,0:T(8,128)(2,1)}) custom-call(bf16[1,128,640]{2,1,0:T(8,128)(2,1)S(1)} %get-tuple-element.4.a, bf16[1,128,640]{2,1,0:T(8,128)(2,1)S(1)} %get-tuple-element.5.b), custom_call_target="tpu_custom_call" | custom-call | tf_op jit(solution)/shard_map/settle/pallas_call | solution.py:362
